TPU v7x, 512 devices: a whole 4x8x8 slice. The times are simulated.
512 devices in a mesh: dp: 8 (over y_hi, core), expert: 64 (over z, x, y_lo).
Axes of the slice: x: 4, y: 8 (y_hi: 4, y_lo: 2; y = y_hi * 2 + y_lo), z: 8, core: 2. Of those that a mesh axis runs over, the one named last changes fastest.
Arguments:
- tokens: bfloat16 [65536, 3584], P(('dp', 'expert')), may hold values from -6 to 6
- cotangent: bfloat16 [65536, 3584], P(('dp', 'expert')), may hold values from -0.59765625 to 0.59765625
- route_ids: int32 [65536, 8], P(('dp', 'expert')), may hold values from 0 to 383, as said below
- gates: bfloat16 [65536, 8], P(('dp', 'expert')), may hold values from 0.099609375 to 1
- w_gate: bfloat16 [64, 3584, 128], P('expert', None, 'dp'), may hold values from -0.09375 to 0.09375
- w_up: bfloat16 [64, 3584, 128], P('expert', None, 'dp'), may hold values from -0.09375 to 0.09375
- w_down: bfloat16 [64, 3584, 128], P('expert', None, 'dp'), may hold values from -0.125 to 0.125
Outputs:
- relaid_gate: bfloat16 [64, 3584, 128], P('expert', 'dp')
- relaid_up: bfloat16 [64, 3584, 128], P('expert', 'dp')
- relaid_down: bfloat16 [64, 3584, 128], P('expert', 'dp')
- grad_gate: float32 [64, 3584, 128], P('expert', 'dp')
- grad_up: float32 [64, 3584, 128], P('expert', 'dp')
- grad_down: float32 [64, 3584, 128], P('expert', 'dp')
- token_grad: bfloat16 [65536, 3584], P(('dp', 'expert'))
- gate_grad: float32 [65536, 8], P(('dp', 'expert'))
Inputs may be any that keep to these rules, and one draw needn't show every extreme that they name: `route_ids`: each row names 8 different experts. Among the 128 rows of one device, at most 6 routes name any one expert below 4; on every device of one index of dp, one same expert below 4 is named by exactly 6 routes.
All inputs are finite; a program needn't handle non-finite values.
Results may differ from a plain program's by a relative error of at most 0.02.
Values may be sent and summed in bfloat16 or wider, within the bound.
No kernel may reach another device: no remote copies, remote signals or barrier semaphores. Data moves between devices by JAX's collectives and lax.ppermute only.
A program may use at most 128 MiB of HBM per device.

v0:
```python
import jax
import jax.numpy as jnp
from jax import lax
from jax.sharding import Mesh
from jax.sharding import PartitionSpec as P

HSPLIT = 16
CAP = 6
PAD = 8
EXPERTS = 4
LANES = 128
DP = ("yh", "core")
BF = jnp.bfloat16
F32 = jnp.float32


def spread(block, axes):
    count = lax.axis_size(axes)
    copies = jnp.broadcast_to(block[None], (count,) + block.shape)
    got = lax.all_to_all(copies, axes, split_axis=0, concat_axis=0, tiled=True)
    return got.reshape((count * block.shape[0],) + block.shape[1:])


def dot(eq, a, b):
    return jnp.einsum(eq, a, b, preferred_element_type=F32)


def shards(tokens, cotangent, route_ids, gates, w_gate, w_up, w_down):
    tok_count, features = tokens.shape
    hidden_dev = w_gate.shape[2]
    mine = jnp.concatenate([w_gate[0].T, w_up[0].T, w_down[0].T], axis=0)
    gathered = lax.all_gather(mine, DP, axis=0, tiled=True)
    n_dp = lax.axis_size(DP)
    ids = route_ids.T
    gates_t = gates.T.astype(F32)
    experts = jnp.arange(EXPERTS, dtype=jnp.int32)
    hits = ids[None] == experts[:, None, None]
    token_hit = jnp.any(hits, axis=1)
    before = (jnp.arange(tok_count)[:, None] < jnp.arange(tok_count)[None, :]).astype(BF)
    rank = dot("et,tu->eu", token_hit.astype(BF), before)
    slots = jnp.arange(PAD, dtype=jnp.int32)
    pick = token_hit[:, None, :] & (rank.astype(jnp.int32)[:, None, :] == slots[None, :, None])
    gate_of = jnp.sum(jnp.where(hits, gates_t[None], 0.0), axis=1)
    gate_slots = jnp.sum(jnp.where(pick, gate_of[:, None, :], 0.0), axis=2)
    pick_rows = pick.reshape(EXPERTS * PAD, tok_count).astype(BF)
    tok_slots = dot("ct,td->cd", pick_rows, tokens).astype(BF)
    cot_slots = dot("ct,td->cd", pick_rows, cotangent).astype(BF)
    gate_cols = jnp.broadcast_to(gate_slots.astype(BF).reshape(-1, 1), (EXPERTS * PAD, LANES))
    rows = jnp.concatenate([tok_slots, gate_cols, cot_slots], axis=1)
    rows = rows.reshape(EXPERTS, PAD, -1)
    rows = lax.all_to_all(rows, "ex", split_axis=0, concat_axis=0, tiled=True)
    rows = rows.reshape(EXPERTS * PAD, -1)
    kept = jnp.arange(EXPERTS * CAP)
    keep = ((kept // CAP * PAD + kept % CAP)[:, None] == jnp.arange(EXPERTS * PAD)[None, :]).astype(
        BF
    )
    wide = features + LANES
    tok_rows = dot("kc,cd->kd", keep, rows[:, :wide]).astype(BF)
    cot_rows = dot("kc,cd->kd", keep, rows[:, wide:]).astype(BF)
    block = EXPERTS * CAP
    tok_half = lax.all_gather(tok_rows, "x", axis=0, tiled=True)
    cot_half = spread(cot_rows, ("zl", "yl"))
    cot_half, gathered = lax.optimization_barrier((cot_half, gathered))
    slot_all = spread(tok_half, ("zl", "yl"))
    slot_cotan = lax.all_gather(cot_half, "x", axis=0, tiled=True)
    slot_tokens = slot_all[:, :features]
    gathered = gathered.reshape(n_dp, 3, hidden_dev, features)

    def reorder(values):
        v = values.reshape(4, 4, block, values.shape[-1])
        return jnp.swapaxes(v, 0, 1).reshape(values.shape)

    slab = [gathered[:, j].reshape(n_dp * hidden_dev, features) for j in range(3)]
    gate_slab, up_slab, down_slab = slab
    pre_gate = reorder(dot("rd,hd->rh", slot_tokens, gate_slab))
    pre_up = reorder(dot("rd,hd->rh", slot_tokens, up_slab))
    slot_gates = reorder(slot_all[:, features : features + 1]).astype(F32)
    sigmoid_gate = jax.nn.sigmoid(pre_gate)
    activation = pre_gate * sigmoid_gate
    hidden = (activation * pre_up).astype(BF)
    back_proj = dot("rd,hd->rh", slot_cotan, down_slab)
    score = jnp.sum(hidden.astype(F32) * back_proj, axis=1, keepdims=True).astype(BF)
    scaled = slot_gates * back_proj
    d_gate = (scaled * pre_up * sigmoid_gate * (1.0 + pre_gate * (1.0 - sigmoid_gate))).astype(BF)
    d_up = (scaled * activation).astype(BF)
    hidden_gated = (slot_gates * hidden.astype(F32)).astype(BF)
    grads = jnp.stack(
        [
            dot("rd,rh->dh", slot_tokens, reorder(d_gate)).astype(BF).reshape(n_dp, -1, LANES),
            dot("rd,rh->dh", slot_tokens, reorder(d_up)).astype(BF).reshape(n_dp, -1, LANES),
            dot("rd,rh->dh", slot_cotan, hidden_gated).astype(BF).reshape(n_dp, -1, LANES),
        ],
        axis=1,
    )
    grads = lax.psum_scatter(grads, DP, scatter_dimension=0, tiled=True)[0].astype(F32)
    left = jnp.concatenate([d_gate, d_up, jnp.broadcast_to(score, d_up.shape)], axis=1)
    first = (jnp.arange(LANES) == 0).astype(BF)[:, None]
    right = jnp.concatenate(
        [
            jnp.concatenate([gate_slab, jnp.zeros((LANES, LANES), BF)], axis=1),
            jnp.concatenate([up_slab, jnp.zeros((LANES, LANES), BF)], axis=1),
            jnp.concatenate(
                [jnp.zeros((LANES, features), BF), jnp.broadcast_to(first, (LANES, LANES))], axis=1
            ),
        ],
        axis=0,
    )
    right = lax.optimization_barrier(right)
    back = dot("rh,hd->rd", left, right).astype(BF)
    back = back.reshape(8, 2 * block, wide)
    back = lax.all_to_all(back, ("x", "zl"), split_axis=0, concat_axis=0, tiled=True)
    back = back.reshape(HSPLIT * block, wide)
    row = jnp.arange(2 * block)
    target = (row // CAP % EXPERTS * 2 + row // block) * PAD + row % CAP
    fold = (jnp.arange(2 * EXPERTS * PAD)[:, None] == target[None, :]).astype(BF)
    home = dot("ck,kd->cd", jnp.tile(fold, (1, 8)), back).astype(BF)
    home = lax.all_to_all(
        home.reshape(2 * EXPERTS, PAD, wide), ("ex", "yl"), split_axis=0, concat_axis=0, tiled=True
    ).reshape(2 * EXPERTS * PAD, wide)
    pick_home = jnp.broadcast_to(pick[:, None], (EXPERTS, 2, PAD, tok_count))
    pick_home = pick_home.reshape(2 * EXPERTS * PAD, tok_count).astype(BF)
    token_grad = dot("ct,cd->td", pick_home, home[:, :features]).astype(BF)
    score_slots = jnp.sum(
        home[:, features : features + 1].astype(F32).reshape(EXPERTS, 2, PAD, 1), axis=1
    )
    score_token = jnp.sum(jnp.where(pick, score_slots, 0.0), axis=1)
    gate_grad = jnp.sum(jnp.where(hits, score_token[:, None, :], 0.0), axis=0).T
    start = lax.axis_index(DP) * (features // n_dp)
    relaid = [lax.dynamic_slice_in_dim(w, start, features // n_dp, axis=1).T[None] for w in slab]
    return (*relaid, grads[0:1], grads[1:2], grads[2:3], token_grad, gate_grad)


def solution(mesh):
    fine = Mesh(mesh.devices.reshape(4, 2, 4, 2, 4, 2), ("yh", "core", "ex", "zl", "x", "yl"))
    expert = ("ex", "zl", "x", "yl")
    rows = P(DP + expert, None)
    weights = P(expert, None, DP)
    laid = P(expert, DP, None)
    return jax.shard_map(
        shards,
        mesh=fine,
        in_specs=(rows,) * 4 + (weights,) * 3,
        out_specs=(laid,) * 6 + (rows,) * 2,
        check_vma=False,
    )
```

profile of v0, /device:TPU:17, one launch (start us, length us, event | category | flops | bytes accessed | tf_op | source)
XLA Modules:
  0.0 203.4 jit_solution(5433098685010183178)
XLA Ops:
  7.2 1.9 pad_maximum_fusion.1
  14.3 10.0 %all-to-all-start = ((bf16[4,8,7296]{2,1,0:T(8,128)(2,1)}), bf16[4,8,7296]{2,1,0:T(8,128)(2,1)S(1)}, u32[]{:S(2)}, u32[]{:S(2)}) async-start(bf16[4,8,7296]{2,1,0:T(8,128)(2,1)} %maximum_bitcast_fusion), calls=%async_computation | async-start | bytes 933888 | tf_op jit(solution)/shard_map/all_to_all | solution.py:51
  24.3 10.8 %all-to-all-done = bf16[4,8,7296]{2,1,0:T(8,128)(2,1)S(1)} async-done(((bf16[4,8,7296]{2,1,0:T(8,128)(2,1)}), bf16[4,8,7296]{2,1,0:T(8,128)(2,1)S(1)}, u32[]{:S(2)}, u32[]{:S(2)}) %all-to-all-start) | async-done | bytes 466976 | tf_op jit(solution)/shard_map/all_to_all | solution.py:51
  36.3 7.7 %all-to-all-start.1 = ((bf16[4,24,3584]{2,1,0:T(8,128)(2,1)}), bf16[4,24,3584]{2,1,0:T(8,128)(2,1)S(1)}, u32[]{:S(2)}, u32[]{:S(2)}) async-start(bf16[4,24,3584]{2,1,0:T(8,128)(2,1)} %broadcast_in_dim.56), calls=%async_computation.1 | async-start | bytes 1376256 | tf_op jit(solution)/shard_map/all_to_all | solution.py:20
  44.2 12.8 %all_gather.10 = bf16[96,3712]{1,0:T(8,128)(2,1)S(1)} all-gather(bf16[24,3712]{1,0:T(8,128)(2,1)S(1)} %convolution_convert_fusion.7), channel_id=1, replica_groups=mesh['yh'=4,'core'=2,'ex'=4,'zl'=2,'x'=4,'yl'=2] {'x'}, dimensions={0}, use_global_device_ids=true | all-gather | bytes 890880 | tf_op jit(solution)/shard_map/all_gather | solution.py:61
  57.0 5.6 %all-to-all-done.1 = bf16[4,24,3584]{2,1,0:T(8,128)(2,1)S(1)} async-done(((bf16[4,24,3584]{2,1,0:T(8,128)(2,1)}), bf16[4,24,3584]{2,1,0:T(8,128)(2,1)S(1)}, u32[]{:S(2)}, u32[]{:S(2)}) %all-to-all-start.1) | async-done | bytes 688160 | tf_op jit(solution)/shard_map/all_to_all | solution.py:20
  62.6 1.8 broadcast_in_dim.64
  64.5 4.6 %all-to-all-start.2 = ((bf16[4,96,3712]{2,1,0:T(8,128)(2,1)}), bf16[4,96,3712]{2,1,0:T(8,128)(2,1)}, u32[]{:S(2)}, u32[]{:S(2)}) async-start(bf16[4,96,3712]{2,1,0:T(8,128)(2,1)} %broadcast_in_dim.64), calls=%async_computation.2 | async-start | bytes 5701632 | tf_op jit(solution)/shard_map/all_to_all | solution.py:20
  69.8 2.8 %fusion.68 = (bf16[8,1,16,3584]{3,2,1,0:T(8,128)(2,1)}, bf16[8,1,16,3584]{3,2,1,0:T(8,128)(2,1)S(1)}, bf16[8,1,16,3584]{3,2,1,0:T(8,128)(2,1)S(1)}) fusion(bf16[8,3,16,3584]{3,2,1,0:T(8,128)(2,1)} %bitcast.154), kind=kLoop, calls=%fused_computation.125 | loop fusion | bytes 5505024 | tf_op jit(solution)/shard_map/slice | solution.py:73
  72.8 6.1 %fusion.9 = bf16[384,3712]{1,0:T(8,128)(2,1)} fusion(bf16[128,128]{1,0:T(8,128)(2,1)S(1)} %broadcast_in_dim.108, bf16[128,3584]{1,0:T(8,128)(2,1)S(1)} %bitcast.147, bf16[128,3584]{1,0:T(8,128)(2,1)S(1)} %bitcast.150), kind=kLoop, calls=%fused_computation.23 | loop fusion | flops 19955712 | bytes 4718592 | tf_op jit(solution)/shard_map/concatenate | solution.py:98
  78.9 22.7 %all-to-all-done.2 = bf16[4,96,3712]{2,1,0:T(8,128)(2,1)} async-done(((bf16[4,96,3712]{2,1,0:T(8,128)(2,1)}), bf16[4,96,3712]{2,1,0:T(8,128)(2,1)}, u32[]{:S(2)}, u32[]{:S(2)}) %all-to-all-start.2) | async-done | bytes 2850848 | tf_op jit(solution)/shard_map/all_to_all | solution.py:20
  101.6 2.0 slice.65
  106.6 7.3 %all-gather.5.cloned.1.call-done = bf16[384,3584]{1,0:T(8,128)(2,1)} async-done(((bf16[96,3584]{1,0:T(8,128)(2,1)}), bf16[384,3584]{1,0:T(8,128)(2,1)}) %all-gather.5.cloned.1.call-update) | async-done | bytes 2752528 | tf_op jit(solution)/shard_map/all_gather | solution.py:65
  113.8 3.0 %fusion.21 = (bf16[384]{0:T(512)(128)(2,1)S(1)}, bf16[384,128]{1,0:T(8,128)(2,1)S(1)}, bf16[384,128]{1,0:T(8,128)(2,1)S(1)}, bf16[384,128]{1,0:T(8,128)(2,1)S(1)}) fusion(f32[4,4,24,128]{3,2,1,0:T(8,128)S(1)} %copy.51, f32[4,4,24,128]{3,2,1,0:T(8,128)S(1)} %copy.52, f32[384]{0:T(512)S(1)} %reshape.223, bf16[384,3584]{1,0:T(8,128)(2,1)} %all-gather.5.cloned.1.call-done, ...), kind=kOutput, calls=%fused_computation.46 | convolution fusion | flops 353255040 | bytes 4360448 | tf_op jit(solution)/shard_map/rd,hd->rh/dot_general | solution.py:25
  116.8 3.8 %convolution_convert_fusion.3 = bf16[3584,128]{1,0:T(8,128)(2,1)} fusion(bf16[384,128]{1,0:T(8,128)(2,1)S(1)} %bitcast.170, bf16[384,3712]{1,0:T(8,128)(2,1)} %bitcast.23), kind=kOutput, calls=%fused_computation.13 | convolution fusion | flops 352780288 | bytes 3768320 | tf_op jit(solution)/shard_map/rd,rh->dh/dot_general | solution.py:25
  120.7 3.2 %convolution_convert_fusion = bf16[384,3712]{1,0:T(8,128)(2,1)} fusion(bf16[384,3712]{1,0:T(8,128)(2,1)S(1)} %copy-done.1, bf16[384,128]{1,0:T(8,128)(2,1)S(1)} %broadcast_in_dim.107, bf16[384,128]{1,0:T(8,128)(2,1)S(1)} %get-tuple-element.53, bf16[384,128]{1,0:T(8,128)(2,1)S(1)} %get-tuple-element.52), kind=kOutput, calls=%fused_computation.10 | convolution fusion | flops 1097023488 | bytes 5996544 | tf_op jit(solution)/shard_map/rh,hd->rd/dot_general | solution.py:25
  124.0 4.4 %all-to-all-start.3 = ((bf16[8,48,3712]{2,1,0:T(8,128)(2,1)}), bf16[8,48,3712]{2,1,0:T(8,128)(2,1)}, u32[]{:S(2)}, u32[]{:S(2)}) async-start(bf16[8,48,3712]{2,1,0:T(8,128)(2,1)} %bitcast.146), calls=%async_computation.4 | async-start | bytes 5701632 | tf_op jit(solution)/shard_map/all_to_all | solution.py:111
  128.6 2.8 %convolution_convert_fusion.2 = bf16[3584,128]{1,0:T(8,128)(2,1)S(1)} fusion(bf16[384,3584]{1,0:T(8,128)(2,1)} %all-gather.5.cloned.1.call-done, bf16[384,128]{1,0:T(8,128)(2,1)S(1)} %get-tuple-element.45, f32[384]{0:T(512)S(1)} %reshape.223), kind=kOutput, calls=%fused_computation.12 | convolution fusion | flops 352927744 | bytes 3769856 | tf_op jit(solution)/shard_map/rd,rh->dh/dot_general | solution.py:25
  131.4 2.8 %convolution_convert_fusion.4 = bf16[3584,128]{1,0:T(8,128)(2,1)S(1)} fusion(bf16[384,128]{1,0:T(8,128)(2,1)S(1)} %bitcast.169, bf16[384,3712]{1,0:T(8,128)(2,1)} %bitcast.23), kind=kOutput, calls=%fused_computation.14 | convolution fusion | flops 352780288 | bytes 3768320 | tf_op jit(solution)/shard_map/rd,rh->dh/dot_general | solution.py:25
  134.2 1.9 pad_maximum_fusion
  136.2 26.7 %all-to-all-done.3 = bf16[8,48,3712]{2,1,0:T(8,128)(2,1)} async-done(((bf16[8,48,3712]{2,1,0:T(8,128)(2,1)}), bf16[8,48,3712]{2,1,0:T(8,128)(2,1)}, u32[]{:S(2)}, u32[]{:S(2)}) %all-to-all-start.3) | async-done | bytes 2850848 | tf_op jit(solution)/shard_map/all_to_all | solution.py:111
  162.9 3.3 %fusion.7 = bf16[8,8,3712]{2,1,0:T(8,128)(2,1)} fusion(bf16[8,48,3712]{2,1,0:T(8,128)(2,1)} %all-to-all-done.3, bf16[64,48]{0,1:T(8,128)(2,1)S(1)} %fusion.33), kind=kOutput, calls=%fused_computation.17 | convolution fusion | flops 182689792 | bytes 3332096 | tf_op jit(solution)/shard_map/ck,kd->cd/dot_general | solution.py:25
  166.2 8.0 %all-to-all-start.4 = ((bf16[8,8,3712]{2,1,0:T(8,128)(2,1)}), bf16[8,8,3712]{2,1,0:T(8,128)(2,1)S(1)}, u32[]{:S(2)}, u32[]{:S(2)}) async-start(bf16[8,8,3712]{2,1,0:T(8,128)(2,1)} %fusion.7), calls=%async_computation.5 | async-start | bytes 950272 | tf_op jit(solution)/shard_map/all_to_all | solution.py:117
  177.7 15.0 %reduce-scatter.2.cloned.1.call-done = bf16[1,3,448,128]{3,2,1,0:T(8,128)(2,1)} async-done(((bf16[8,3,448,128]{3,2,1,0:T(8,128)(2,1)}), bf16[1,3,448,128]{3,2,1,0:T(8,128)(2,1)}) %reduce-scatter.2.cloned.1.call-update) | async-done | bytes 344080 | tf_op jit(solution)/shard_map/reduce_scatter | solution.py:95
  (62 shorter events, 18.5 us)
Async XLA Ops:
  7.2 4.4 %copy-start = (bf16[128,3584]{1,0:T(8,128)(2,1)S(1)}, bf16[128,3584]{1,0:T(8,128)(2,1)}, u32[]{:S(2)}) copy-start(bf16[128,3584]{1,0:T(8,128)(2,1)} %param.8) | copy-start | bytes 2752516
  7.2 62.0 %all-gather.3.cloned.1.call-start = ((), (), s32[]{:S(2)}) async-start(), calls=%async_computation.6 | async-start | bytes 3096576 | tf_op jit(solution)/shard_map/all_gather | solution.py:32
  14.3 20.9 %all-to-all-start = ((bf16[4,8,7296]{2,1,0:T(8,128)(2,1)}), bf16[4,8,7296]{2,1,0:T(8,128)(2,1)S(1)}, u32[]{:S(2)}, u32[]{:S(2)}) async-start(bf16[4,8,7296]{2,1,0:T(8,128)(2,1)} %maximum_bitcast_fusion), calls=%async_computation | async-start | bytes 933888 | tf_op jit(solution)/shard_map/all_to_all | solution.py:51
  36.3 26.4 %all-to-all-start.1 = ((bf16[4,24,3584]{2,1,0:T(8,128)(2,1)}), bf16[4,24,3584]{2,1,0:T(8,128)(2,1)S(1)}, u32[]{:S(2)}, u32[]{:S(2)}) async-start(bf16[4,24,3584]{2,1,0:T(8,128)(2,1)} %broadcast_in_dim.56), calls=%async_computation.1 | async-start | bytes 1376256 | tf_op jit(solution)/shard_map/all_to_all | solution.py:20
  62.6 1.8 copy-start.2
  64.5 37.1 %all-to-all-start.2 = ((bf16[4,96,3712]{2,1,0:T(8,128)(2,1)}), bf16[4,96,3712]{2,1,0:T(8,128)(2,1)}, u32[]{:S(2)}, u32[]{:S(2)}) async-start(bf16[4,96,3712]{2,1,0:T(8,128)(2,1)} %broadcast_in_dim.64), calls=%async_computation.2 | async-start | bytes 5701632 | tf_op jit(solution)/shard_map/all_to_all | solution.py:20
  69.1 44.7 %all-gather.5.cloned.1.call-start = ((), (), s32[]{:S(2)}) async-start(), calls=%async_computation.7 | async-start | bytes 3440640 | tf_op jit(solution)/shard_map/all_gather | solution.py:65
  116.8 3.9 %copy-start.1 = (bf16[384,3712]{1,0:T(8,128)(2,1)S(1)}, bf16[384,3712]{1,0:T(8,128)(2,1)}, u32[]{:S(2)}) copy-start(bf16[384,3712]{1,0:T(8,128)(2,1)} %fusion.9) | copy-start | bytes 8552452
  124.0 38.9 %all-to-all-start.3 = ((bf16[8,48,3712]{2,1,0:T(8,128)(2,1)}), bf16[8,48,3712]{2,1,0:T(8,128)(2,1)}, u32[]{:S(2)}, u32[]{:S(2)}) async-start(bf16[8,48,3712]{2,1,0:T(8,128)(2,1)} %bitcast.146), calls=%async_computation.4 | async-start | bytes 5701632 | tf_op jit(solution)/shard_map/all_to_all | solution.py:111
  128.4 64.3 %reduce-scatter.2.cloned.1.call-start = ((), (), s32[]{:S(2)}) async-start(), calls=%async_computation.8 | async-start | bytes 3096576 | tf_op jit(solution)/shard_map/reduce_scatter | solution.py:95
  131.4 2.8 %copy-start.3 = (bf16[3584,128]{1,0:T(8,128)(2,1)S(1)}, bf16[3584,128]{1,0:T(8,128)(2,1)}, u32[]{:S(2)}) copy-start(bf16[3584,128]{1,0:T(8,128)(2,1)} %convolution_convert_fusion.3) | copy-start | bytes 2752516
  166.2 28.4 %all-to-all-start.4 = ((bf16[8,8,3712]{2,1,0:T(8,128)(2,1)}), bf16[8,8,3712]{2,1,0:T(8,128)(2,1)S(1)}, u32[]{:S(2)}, u32[]{:S(2)}) async-start(bf16[8,8,3712]{2,1,0:T(8,128)(2,1)} %fusion.7), calls=%async_computation.5 | async-start | bytes 950272 | tf_op jit(solution)/shard_map/all_to_all | solution.py:117
  174.2 22.0 %copy-start.4 = (s32[128,8]{0,1:T(8,128)S(1)}, s32[128,8]{0,1:T(8,128)}, u32[]{:S(2)}) copy-start(s32[128,8]{0,1:T(8,128)} %param.9) | copy-start | bytes 12292
Sparse Core Ops, SparseCore 0:
  10.1 51.8 all-gather.2
  72.0 41.7 all-gather.4
  136.2 56.4 reduce-scatter.1
where the time goes:
time: 204 us; the launch traced here: 203 us
  waiting for transfers between devices  88.8 us (44%)
  starting transfers between devices  35 us (17%)
  matrix products  24.3 us (12%)
  other arithmetic  15.8 us (8%)
  between operations  14 us (7%)
  blocking collectives  12.8 us (6%)
  local copies, waits for them, and re-layouts  12.7 us (6%)
    all_to_all x2, waiting for transfers between devices, spread(): got = lax.all_to_all(copies, axes, split_axis=0, concat_axis=0, tiled=True)  28.3 us
    all_to_all x1, waiting for transfers between devices, shards(): lax.all_to_all(back, ('x', 'zl'), split_axis=0, concat_axis=0, tiled=True)  26.7 us
    dot_general x14, matrix products, dot(): return jnp.einsum(eq, a, b, preferred_element_type=F32)  24.3 us
    reduce_scatter x1, waiting for transfers between devices, shards(): lax.psum_scatter(grads, DP, scatter_dimension=0, tiled=True)[0].astype(F32)  15 us
    all_gather x1, blocking collectives, shards(): tok_half = lax.all_gather(tok_rows, 'x', axis=0, tiled=True)  12.8 us
    all_to_all x2, starting transfers between devices, spread(): got = lax.all_to_all(copies, axes, split_axis=0, concat_axis=0, tiled=True)  12.2 us
    all_to_all x1, waiting for transfers between devices, shards(): rows = lax.all_to_all(rows, 'ex', split_axis=0, concat_axis=0, tiled=True)  10.8 us
    all_to_all x1, starting transfers between devices, shards(): rows = lax.all_to_all(rows, 'ex', split_axis=0, concat_axis=0, tiled=True)  10 us
  transfers between devices with their start and end apart: 8, of which 6 were waited for; matrix products, arithmetic and copies ran while one was open for 19% of the time, Pallas kernels for 0%

commit v1 on v0

--- a/solution.py
+++ b/solution.py
@@ -62,7 +62,10 @@
     cot_half = spread(cot_rows, ("zl", "yl"))
     cot_half, gathered = lax.optimization_barrier((cot_half, gathered))
     slot_all = spread(tok_half, ("zl", "yl"))
-    slot_cotan = lax.all_gather(cot_half, "x", axis=0, tiled=True)
+    size = lax.axis_size("x")
+    parts = jnp.stack([cot_half for _ in range(size)])
+    parts = lax.all_to_all(parts, "x", split_axis=0, concat_axis=0)
+    slot_cotan = jnp.concatenate(parts, axis=0)
     slot_tokens = slot_all[:, :features]
     gathered = gathered.reshape(n_dp, 3, hidden_dev, features)
 

time: 204 us -> 244 us (1.20)
  the two profiles are of different devices: /device:TPU:17 before, /device:TPU:1 now
where the time goes in v1:
time: 244 us; the launch traced here: 243 us
  waiting for transfers between devices  120 us (49%)
  starting transfers between devices  39 us (16%)
  matrix products  26.1 us (11%)
  local copies, waits for them, and re-layouts  16.2 us (7%)
  other arithmetic  14.7 us (6%)
  between operations  14.4 us (6%)
  blocking collectives  12.2 us (5%)
    all_gather x1, waiting for transfers between devices, shards(): gathered = lax.all_gather(mine, DP, axis=0, tiled=True)  34.5 us
    all_to_all x1, waiting for transfers between devices, shards(): lax.all_to_all(back, ('x', 'zl'), split_axis=0, concat_axis=0, tiled=True)  28.2 us
    dot_general x14, matrix products, dot(): return jnp.einsum(eq, a, b, preferred_element_type=F32)  26.1 us
    all_to_all x2, waiting for transfers between devices, spread(): got = lax.all_to_all(copies, axes, split_axis=0, concat_axis=0, tiled=True)  17.3 us
    all_to_all x1, waiting for transfers between devices, shards(): parts = lax.all_to_all(parts, 'x', split_axis=0, concat_axis=0)  14.8 us
    reduce_scatter x1, waiting for transfers between devices, shards(): lax.psum_scatter(grads, DP, scatter_dimension=0, tiled=True)[0].astype(F32)  14.6 us
    all_to_all x2, starting transfers between devices, spread(): got = lax.all_to_all(copies, axes, split_axis=0, concat_axis=0, tiled=True)  12.2 us
    all_gather x1, blocking collectives, shards(): tok_half = lax.all_gather(tok_rows, 'x', axis=0, tiled=True)  12.2 us
  transfers between devices with their start and end apart: 8, of which 6 were waited for; matrix products, arithmetic and copies ran while one was open for 14% of the time, Pallas kernels for 0%

profile of v1, /device:TPU:1, one launch (start us, length us, event | category | flops | bytes accessed | tf_op | source)
XLA Modules:
  0.0 242.9 jit_solution(1743656335894108593)
XLA Ops:
  12.5 10.8 %all-to-all-start = ((bf16[4,8,7296]{2,1,0:T(8,128)(2,1)}), bf16[4,8,7296]{2,1,0:T(8,128)(2,1)S(1)}, u32[]{:S(2)}, u32[]{:S(2)}) async-start(bf16[4,8,7296]{2,1,0:T(8,128)(2,1)} %maximum_bitcast_fusion), calls=%async_computation | async-start | bytes 933888 | tf_op jit(solution)/shard_map/all_to_all | solution.py:51
  23.3 10.8 %all-to-all-done = bf16[4,8,7296]{2,1,0:T(8,128)(2,1)S(1)} async-done(((bf16[4,8,7296]{2,1,0:T(8,128)(2,1)}), bf16[4,8,7296]{2,1,0:T(8,128)(2,1)S(1)}, u32[]{:S(2)}, u32[]{:S(2)}) %all-to-all-start) | async-done | bytes 466976 | tf_op jit(solution)/shard_map/all_to_all | solution.py:51
  35.3 7.6 %all-to-all-start.1 = ((bf16[4,24,3584]{2,1,0:T(8,128)(2,1)}), bf16[4,24,3584]{2,1,0:T(8,128)(2,1)S(1)}, u32[]{:S(2)}, u32[]{:S(2)}) async-start(bf16[4,24,3584]{2,1,0:T(8,128)(2,1)} %broadcast_in_dim.56), calls=%async_computation.1 | async-start | bytes 1376256 | tf_op jit(solution)/shard_map/all_to_all | solution.py:20
  43.9 12.2 %all_gather.7 = bf16[96,3712]{1,0:T(8,128)(2,1)S(1)} all-gather(bf16[24,3712]{1,0:T(8,128)(2,1)S(1)} %convolution_convert_fusion.7), channel_id=1, replica_groups=mesh['yh'=4,'core'=2,'ex'=4,'zl'=2,'x'=4,'yl'=2] {'x'}, dimensions={0}, use_global_device_ids=true | all-gather | bytes 890880 | tf_op jit(solution)/shard_map/all_gather | solution.py:61
  57.9 4.6 %all-to-all-start.2 = ((bf16[4,96,3712]{2,1,0:T(8,128)(2,1)}), bf16[4,96,3712]{2,1,0:T(8,128)(2,1)}, u32[]{:S(2)}, u32[]{:S(2)}) async-start(bf16[4,96,3712]{2,1,0:T(8,128)(2,1)} %broadcast_in_dim.64), calls=%async_computation.2 | async-start | bytes 5701632 | tf_op jit(solution)/shard_map/all_to_all | solution.py:20
  62.6 34.5 %all-gather.2.cloned.1.call-done = bf16[384,3584]{1,0:T(8,128)(2,1)} async-done(((bf16[48,3584]{1,0:T(8,128)(2,1)}), bf16[384,3584]{1,0:T(8,128)(2,1)}) %all-gather.2.cloned.1.call-update) | async-done | bytes 2752528 | tf_op jit(solution)/shard_map/all_gather | solution.py:32
  97.1 17.3 %all-to-all-done.2 = bf16[4,96,3712]{2,1,0:T(8,128)(2,1)} async-done(((bf16[4,96,3712]{2,1,0:T(8,128)(2,1)}), bf16[4,96,3712]{2,1,0:T(8,128)(2,1)}, u32[]{:S(2)}, u32[]{:S(2)}) %all-to-all-start.2) | async-done | bytes 2850848 | tf_op jit(solution)/shard_map/all_to_all | solution.py:20
  114.4 1.9 stack.4
  116.2 4.6 %all-to-all-start.3 = ((bf16[4,96,3584]{2,1,0:T(8,128)(2,1)}), bf16[4,96,3584]{2,1,0:T(8,128)(2,1)}, u32[]{:S(2)}, u32[]{:S(2)}) async-start(bf16[4,96,3584]{2,1,0:T(8,128)(2,1)} %stack.4), calls=%async_computation.3 | async-start | bytes 5505024 | tf_op jit(solution)/shard_map/all_to_all | solution.py:67
  120.8 2.8 %fusion.63 = (bf16[8,1,16,3584]{3,2,1,0:T(8,128)(2,1)}, bf16[8,1,16,3584]{3,2,1,0:T(8,128)(2,1)S(1)}, bf16[8,1,16,3584]{3,2,1,0:T(8,128)(2,1)S(1)}) fusion(bf16[8,3,16,3584]{3,2,1,0:T(8,128)(2,1)} %bitcast.159), kind=kLoop, calls=%fused_computation.123 | loop fusion | bytes 5505024 | tf_op jit(solution)/shard_map/slice | solution.py:76
  123.8 6.1 %fusion.9 = bf16[384,3712]{1,0:T(8,128)(2,1)} fusion(bf16[128,128]{1,0:T(8,128)(2,1)S(1)} %broadcast_in_dim.108, bf16[128,3584]{1,0:T(8,128)(2,1)S(1)} %bitcast.156, bf16[128,3584]{1,0:T(8,128)(2,1)S(1)} %bitcast.152), kind=kLoop, calls=%fused_computation.23 | loop fusion | flops 19955712 | bytes 4718592 | tf_op jit(solution)/shard_map/concatenate | solution.py:101
  129.9 3.5 %slice.65 = bf16[384,3584]{1,0:T(8,128)(2,1)} slice(bf16[384,3712]{1,0:T(8,128)(2,1)} %bitcast.23), slice={[0:384], [0:3584]} | slice | bytes 5505024 | tf_op jit(solution)/shard_map/slice | solution.py:69
  134.6 2.8 %convolution_bitcast_fusion.1 = f32[4,4,24,128]{3,2,0,1:T(8,128)S(1)} fusion(bf16[4,4,24,3584]{3,2,1,0:T(8,128)(2,1)} %bitcast.150, bf16[128,3584,1,1]{1,0,3,2:T(8,128)(2,1)S(1)} %bitcast.153), kind=kOutput, calls=%fused_computation.25 | convolution fusion | flops 352321536 | bytes 3866624 | tf_op jit(solution)/shard_map/rd,hd->rh/dot_general | solution.py:25
  138.5 14.8 %all-to-all-done.3 = bf16[4,96,3584]{2,1,0:T(8,128)(2,1)} async-done(((bf16[4,96,3584]{2,1,0:T(8,128)(2,1)}), bf16[4,96,3584]{2,1,0:T(8,128)(2,1)}, u32[]{:S(2)}, u32[]{:S(2)}) %all-to-all-start.3) | async-done | bytes 2752544 | tf_op jit(solution)/shard_map/all_to_all | solution.py:67
  153.3 2.8 %convolution_convert_fusion.2 = bf16[3584,128]{1,0:T(8,128)(2,1)S(1)} fusion(bf16[384,3584]{1,0:T(8,128)(2,1)} %bitcast.25, bf16[384,128]{1,0:T(8,128)(2,1)S(1)} %bitcast.169), kind=kOutput, calls=%fused_computation.12 | convolution fusion | flops 352780288 | bytes 3768320 | tf_op jit(solution)/shard_map/rd,rh->dh/dot_general | solution.py:25
  156.1 2.7 %multiply_reduce_fusion = (bf16[384]{0:T(512)(128)(2,1)S(1)}, bf16[384,128]{1,0:T(8,128)(2,1)S(1)}, bf16[384,128]{1,0:T(8,128)(2,1)S(1)}) fusion(f32[4,4,24,128]{3,2,1,0:T(8,128)S(1)} %copy.53, f32[4,4,24,128]{3,2,1,0:T(8,128)S(1)} %copy.54, f32[384]{0:T(512)S(1)} %reshape.240, bf16[384,3584]{1,0:T(8,128)(2,1)} %bitcast.25, bf16[128,3584]{1,0:T(8,128)(2,1)S(1)} %bitcast.166), kind=kOutput, calls=%fused_computation.57 | convolution fusion | flops 353255040 | bytes 4262144 | tf_op jit(solution)/shard_map/rd,hd->rh/dot_general | solution.py:25
  158.8 3.9 %convolution_convert_fusion.3 = bf16[3584,128]{1,0:T(8,128)(2,1)} fusion(bf16[384,128]{1,0:T(8,128)(2,1)S(1)} %bitcast.176, bf16[384,3712]{1,0:T(8,128)(2,1)} %bitcast.23), kind=kOutput, calls=%fused_computation.13 | convolution fusion | flops 352780288 | bytes 3768320 | tf_op jit(solution)/shard_map/rd,rh->dh/dot_general | solution.py:25
  162.8 3.2 %convolution_convert_fusion = bf16[384,3712]{1,0:T(8,128)(2,1)} fusion(bf16[384,3712]{1,0:T(8,128)(2,1)S(1)} %copy-done.1, bf16[384,128]{1,0:T(8,128)(2,1)S(1)} %broadcast_in_dim.107, bf16[384,128]{1,0:T(8,128)(2,1)S(1)} %get-tuple-element.52, bf16[384,128]{1,0:T(8,128)(2,1)S(1)} %get-tuple-element.51), kind=kOutput, calls=%fused_computation.10 | convolution fusion | flops 1097023488 | bytes 5996544 | tf_op jit(solution)/shard_map/rh,hd->rd/dot_general | solution.py:25
  166.1 4.4 %all-to-all-start.4 = ((bf16[8,48,3712]{2,1,0:T(8,128)(2,1)}), bf16[8,48,3712]{2,1,0:T(8,128)(2,1)}, u32[]{:S(2)}, u32[]{:S(2)}) async-start(bf16[8,48,3712]{2,1,0:T(8,128)(2,1)} %bitcast.149), calls=%async_computation.5 | async-start | bytes 5701632 | tf_op jit(solution)/shard_map/all_to_all | solution.py:114
  170.7 2.8 %convolution_convert_fusion.4 = bf16[3584,128]{1,0:T(8,128)(2,1)S(1)} fusion(bf16[384,128]{1,0:T(8,128)(2,1)S(1)} %bitcast.175, bf16[384,3712]{1,0:T(8,128)(2,1)} %bitcast.23), kind=kOutput, calls=%fused_computation.14 | convolution fusion | flops 352780288 | bytes 3768320 | tf_op jit(solution)/shard_map/rd,rh->dh/dot_general | solution.py:25
  175.5 28.2 %all-to-all-done.4 = bf16[8,48,3712]{2,1,0:T(8,128)(2,1)} async-done(((bf16[8,48,3712]{2,1,0:T(8,128)(2,1)}), bf16[8,48,3712]{2,1,0:T(8,128)(2,1)}, u32[]{:S(2)}, u32[]{:S(2)}) %all-to-all-start.4) | async-done | bytes 2850848 | tf_op jit(solution)/shard_map/all_to_all | solution.py:114
  203.7 3.2 %fusion.7 = bf16[8,8,3712]{2,1,0:T(8,128)(2,1)} fusion(bf16[8,48,3712]{2,1,0:T(8,128)(2,1)} %all-to-all-done.4, bf16[64,48]{0,1:T(8,128)(2,1)S(1)} %fusion.29), kind=kOutput, calls=%fused_computation.17 | convolution fusion | flops 182689792 | bytes 3332096 | tf_op jit(solution)/shard_map/ck,kd->cd/dot_general | solution.py:25
  206.9 6.8 %all-to-all-start.5 = ((bf16[8,8,3712]{2,1,0:T(8,128)(2,1)}), bf16[8,8,3712]{2,1,0:T(8,128)(2,1)S(1)}, u32[]{:S(2)}, u32[]{:S(2)}) async-start(bf16[8,8,3712]{2,1,0:T(8,128)(2,1)} %fusion.7), calls=%async_computation.6 | async-start | bytes 950272 | tf_op jit(solution)/shard_map/all_to_all | solution.py:120
  217.2 14.6 %reduce-scatter.2.cloned.1.call-done = bf16[1,3,448,128]{3,2,1,0:T(8,128)(2,1)} async-done(((bf16[8,3,448,128]{3,2,1,0:T(8,128)(2,1)}), bf16[1,3,448,128]{3,2,1,0:T(8,128)(2,1)}) %reduce-scatter.2.cloned.1.call-update) | async-done | bytes 344080 | tf_op jit(solution)/shard_map/reduce_scatter | solution.py:98
  (73 shorter events, 21.5 us)
Async XLA Ops:
  7.2 2.6 %copy-start = (bf16[128,3584]{1,0:T(8,128)(2,1)S(1)}, bf16[128,3584]{1,0:T(8,128)(2,1)}, u32[]{:S(2)}) copy-start(bf16[128,3584]{1,0:T(8,128)(2,1)} %param.8) | copy-start | bytes 2752516
  10.0 32.8 %copy-start.6 = (bf16[1,3584,16]{1,2,0:T(8,128)(2,1)S(1)}, bf16[1,3584,16]{1,2,0:T(8,128)(2,1)}, u32[]{:S(2)}) copy-start(bf16[1,3584,16]{1,2,0:T(8,128)(2,1)} %param.13) | copy-start | bytes 344068
  10.1 32.8 %copy-start.7 = (bf16[1,3584,16]{1,2,0:T(8,128)(2,1)S(1)}, bf16[1,3584,16]{1,2,0:T(8,128)(2,1)}, u32[]{:S(2)}) copy-start(bf16[1,3584,16]{1,2,0:T(8,128)(2,1)} %param.12) | copy-start | bytes 344068
  10.1 32.8 %copy-start.8 = (bf16[1,3584,16]{1,2,0:T(8,128)(2,1)S(1)}, bf16[1,3584,16]{1,2,0:T(8,128)(2,1)}, u32[]{:S(2)}) copy-start(bf16[1,3584,16]{1,2,0:T(8,128)(2,1)} %param.11) | copy-start | bytes 344068
  12.5 21.7 %all-to-all-start = ((bf16[4,8,7296]{2,1,0:T(8,128)(2,1)}), bf16[4,8,7296]{2,1,0:T(8,128)(2,1)S(1)}, u32[]{:S(2)}, u32[]{:S(2)}) async-start(bf16[4,8,7296]{2,1,0:T(8,128)(2,1)} %maximum_bitcast_fusion), calls=%async_computation | async-start | bytes 933888 | tf_op jit(solution)/shard_map/all_to_all | solution.py:51
  35.3 20.8 %all-to-all-start.1 = ((bf16[4,24,3584]{2,1,0:T(8,128)(2,1)}), bf16[4,24,3584]{2,1,0:T(8,128)(2,1)S(1)}, u32[]{:S(2)}, u32[]{:S(2)}) async-start(bf16[4,24,3584]{2,1,0:T(8,128)(2,1)} %broadcast_in_dim.56), calls=%async_computation.1 | async-start | bytes 1376256 | tf_op jit(solution)/shard_map/all_to_all | solution.py:20
  42.9 54.2 %all-gather.2.cloned.1.call-start = ((), (), s32[]{:S(2)}) async-start(), calls=%async_computation.7 | async-start | bytes 3096576 | tf_op jit(solution)/shard_map/all_gather | solution.py:32
  57.9 56.5 %all-to-all-start.2 = ((bf16[4,96,3712]{2,1,0:T(8,128)(2,1)}), bf16[4,96,3712]{2,1,0:T(8,128)(2,1)}, u32[]{:S(2)}, u32[]{:S(2)}) async-start(bf16[4,96,3712]{2,1,0:T(8,128)(2,1)} %broadcast_in_dim.64), calls=%async_computation.2 | async-start | bytes 5701632 | tf_op jit(solution)/shard_map/all_to_all | solution.py:20
  116.2 37.0 %all-to-all-start.3 = ((bf16[4,96,3584]{2,1,0:T(8,128)(2,1)}), bf16[4,96,3584]{2,1,0:T(8,128)(2,1)}, u32[]{:S(2)}, u32[]{:S(2)}) async-start(bf16[4,96,3584]{2,1,0:T(8,128)(2,1)} %stack.4), calls=%async_computation.3 | async-start | bytes 5505024 | tf_op jit(solution)/shard_map/all_to_all | solution.py:67
  123.7 13.7 %copy-start.3 = (bf16[8,1,16,3584]{3,2,1,0:T(8,128)(2,1)}, bf16[8,1,16,3584]{3,2,1,0:T(8,128)(2,1)S(1)}, u32[]{:S(2)}) copy-start(bf16[8,1,16,3584]{3,2,1,0:T(8,128)(2,1)S(1)} %get-tuple-element.45) | copy-start | bytes 2752516
  134.5 2.8 %copy-start.2 = (bf16[384,3584]{1,0:T(8,128)(2,1)S(1)}, bf16[384,3584]{1,0:T(8,128)(2,1)}, u32[]{:S(2)}) copy-start(bf16[384,3584]{1,0:T(8,128)(2,1)} %slice.65) | copy-start | bytes 8257540
  153.3 2.8 %copy-start.4 = (bf16[8,1,16,3584]{3,2,1,0:T(8,128)(2,1)S(1)}, bf16[8,1,16,3584]{3,2,1,0:T(8,128)(2,1)}, u32[]{:S(2)}) copy-start(bf16[8,1,16,3584]{3,2,1,0:T(8,128)(2,1)} %get-tuple-element.44) | copy-start | bytes 2752516
  158.8 4.0 %copy-start.1 = (bf16[384,3712]{1,0:T(8,128)(2,1)S(1)}, bf16[384,3712]{1,0:T(8,128)(2,1)}, u32[]{:S(2)}) copy-start(bf16[384,3712]{1,0:T(8,128)(2,1)} %fusion.9) | copy-start | bytes 8552452
  166.1 37.6 %all-to-all-start.4 = ((bf16[8,48,3712]{2,1,0:T(8,128)(2,1)}), bf16[8,48,3712]{2,1,0:T(8,128)(2,1)}, u32[]{:S(2)}, u32[]{:S(2)}) async-start(bf16[8,48,3712]{2,1,0:T(8,128)(2,1)} %bitcast.149), calls=%async_computation.5 | async-start | bytes 5701632 | tf_op jit(solution)/shard_map/all_to_all | solution.py:114
  170.5 61.4 %reduce-scatter.2.cloned.1.call-start = ((), (), s32[]{:S(2)}) async-start(), calls=%async_computation.8 | async-start | bytes 3096576 | tf_op jit(solution)/shard_map/reduce_scatter | solution.py:98
  170.7 2.8 %copy-start.5 = (bf16[3584,128]{1,0:T(8,128)(2,1)S(1)}, bf16[3584,128]{1,0:T(8,128)(2,1)}, u32[]{:S(2)}) copy-start(bf16[3584,128]{1,0:T(8,128)(2,1)} %convolution_convert_fusion.3) | copy-start | bytes 2752516
  206.9 26.8 %all-to-all-start.5 = ((bf16[8,8,3712]{2,1,0:T(8,128)(2,1)}), bf16[8,8,3712]{2,1,0:T(8,128)(2,1)S(1)}, u32[]{:S(2)}, u32[]{:S(2)}) async-start(bf16[8,8,3712]{2,1,0:T(8,128)(2,1)} %fusion.7), calls=%async_computation.6 | async-start | bytes 950272 | tf_op jit(solution)/shard_map/all_to_all | solution.py:120
  213.6 21.7 %copy-start.9 = (s32[128,8]{0,1:T(8,128)S(1)}, s32[128,8]{0,1:T(8,128)}, u32[]{:S(2)}) copy-start(s32[128,8]{0,1:T(8,128)} %param.9) | copy-start | bytes 12292
Sparse Core Ops, SparseCore 0:
  45.8 51.2 all-gather.1
  175.5 56.2 reduce-scatter.1
